TPU v7x, 128 devices: a whole 4x4x4 slice. The times are simulated.
128 devices in a mesh: comp: 4 (over x), blk: 32 (over y, z, core).
Axes of the slice: x: 4, y: 4, z: 4, core: 2. Of those that a mesh axis runs over, the one named last changes fastest.
Arguments:
- psi_start: float32 [4, 6, 256, 128, 128], P('comp', None, 'blk'), may hold values from -6 to 6
- adj_source: float32 [4, 6, 256, 128, 128], P('comp', None, 'blk'), may hold values from -6 to 6
- vol_inverse: float32 [4, 256, 128, 128], P('comp', 'blk'), may hold values from 0.5 to 2
- coupling: float32 [4, 6, 6, 6], P('comp'), may hold values from -0.6 to 0.65
- send_tile: int32 [128, 128, 8], P(('comp', 'blk')), may hold values from 0 to 1023
- send_count: int32 [128, 128], P(('comp', 'blk')), may hold values from 0 to 8, as said below
- send_weight: float32 [128, 128, 8], P(('comp', 'blk')), may hold values from 0.2 to 1
- recv_slot: int32 [128, 128, 8], P(('comp', 'blk')), may hold values from 0 to 63
- fringe_row: int32 [128, 64], P(('comp', 'blk')), may hold values from 0 to 1023, as said below
Outputs:
- psi_end: float32 [4, 6, 256, 128, 128], P('comp', None, 'blk')
Inputs may be any that keep to these rules, and one draw needn't show every extreme that they name: `send_count`: no tiles travel between devices of the same component; between devices of different components the count is 4 or more. In every draw one receiver gets 8 live entries from every device of the other components. `fringe_row`: the rows of one device's fringe slots are distinct.
All inputs are finite; a program needn't handle non-finite values.
Results may differ from a plain program's by a relative error of at most 0.0003.
Values sent between devices are 32-bit elements; how exact they have to be, the bound alone decides.
No kernel may reach another device: no remote copies, remote signals or barrier semaphores. Data moves between devices by JAX's collectives and lax.ppermute only.
A program may use at most 128 MiB of HBM per device.

v0:
```python
import jax
import jax.numpy as jnp
from jax import lax
from jax.sharding import PartitionSpec as P

PENALTY = 4.0
TIME_STEP = 0.08


def padded(cells, sides, width):
    for axis, dim in sides:
        count = lax.axis_size(axis)
        ends = count - 1
        head = lax.slice_in_dim(cells, 0, width, axis=dim)
        tail = lax.slice_in_dim(cells, cells.shape[dim] - width, cells.shape[dim], axis=dim)
        cells = jnp.concatenate(
            [
                lax.ppermute(tail, axis, [(i, (i + 1) % count) for i in range(ends)]),
                cells,
                lax.ppermute(head, axis, [((i + 1) % count, i) for i in range(ends)]),
            ],
            axis=dim,
        )
    return cells


def fringe_values(field, send_tile, send_count, send_weight, recv_slot, count_slots):
    nvar, depth, width, length = field.shape
    flat = field.reshape(nvar, depth * width, length)
    peers, capacity = send_tile.shape
    picked = jnp.take(flat, send_tile.reshape(-1), axis=1)
    live = lax.broadcasted_iota(jnp.int32, (peers, capacity), 1) < send_count.reshape(peers, 1)
    scale = jnp.where(live, send_weight, 0.0).reshape(-1)
    outgoing = (picked * scale[None, :, None]).reshape(nvar, peers, capacity, length)
    arrived = lax.all_to_all(outgoing, ("comp", "blk"), split_axis=1, concat_axis=1, tiled=True)
    arrived = arrived.reshape(nvar, peers * capacity, length)
    slot_ids = lax.broadcasted_iota(jnp.int32, (count_slots, 1), 0)
    onehot = (recv_slot.reshape(1, -1) == slot_ids).astype(jnp.float32)
    return jnp.einsum("sk,vkz->vsz", onehot, arrived, precision=lax.Precision.HIGHEST)


def apply_block(matrix, values):
    return jnp.einsum("vu,vxyz->uxyz", matrix, values, precision=lax.Precision.HIGHEST)


def residual_of(field, volume, source, matrices, interp, rows):
    nvar, depth, width, length = field.shape
    extended = padded(field, (("blk", 1),), 1)
    zero_y = jnp.zeros((nvar, depth, 1, length), jnp.float32)
    zero_z = jnp.zeros((nvar, depth, width, 1), jnp.float32)
    flux = apply_block(-jnp.sum(matrices, axis=0), field)
    flux = flux + apply_block(matrices[0], extended[:, 2:])
    flux = flux + apply_block(matrices[1], extended[:, :-2])
    flux = flux + apply_block(matrices[2], jnp.concatenate([field[:, :, 1:], zero_y], axis=2))
    flux = flux + apply_block(matrices[3], jnp.concatenate([zero_y, field[:, :, :-1]], axis=2))
    flux = flux + apply_block(matrices[4], jnp.concatenate([field[:, :, :, 1:], zero_z], axis=3))
    flux = flux + apply_block(matrices[5], jnp.concatenate([zero_z, field[:, :, :, :-1]], axis=3))
    rate = volume[None] * flux + source
    rate_flat = rate.reshape(nvar, depth * width, length)
    field_flat = field.reshape(nvar, depth * width, length)
    rate_flat = rate_flat.at[:, rows, :].add(PENALTY * (interp - field_flat[:, rows, :]))
    return rate_flat.reshape(nvar, depth, width, length)


def shards(
    psi_start,
    adj_source,
    vol_inverse,
    coupling,
    send_tile,
    send_count,
    send_weight,
    recv_slot,
    fringe_row,
):
    start = psi_start[0]
    source = adj_source[0]
    volume = vol_inverse[0]
    matrices = coupling[0]
    rows = fringe_row[0]

    def rate_of(field):
        interp = fringe_values(
            field, send_tile[0], send_count[0], send_weight[0], recv_slot[0], rows.shape[0]
        )
        return residual_of(field, volume, source, matrices, interp, rows)

    first = rate_of(start)
    middle = start + TIME_STEP * first
    second = rate_of(middle)
    result = start + 0.5 * TIME_STEP * (first + second)
    return result[None]


def solution(mesh):
    in_specs = (
        P("comp", None, "blk", None, None),
        P("comp", None, "blk", None, None),
        P("comp", "blk", None, None),
        P("comp", None, None, None),
        P(("comp", "blk"), None, None),
        P(("comp", "blk"), None),
        P(("comp", "blk"), None, None),
        P(("comp", "blk"), None, None),
        P(("comp", "blk"), None),
    )
    out_specs = P("comp", None, "blk", None, None)
    return jax.shard_map(shards, mesh=mesh, in_specs=in_specs, out_specs=out_specs, check_vma=False)
```

profile of v0, /device:TPU:1, one launch (start us, length us, event | category | flops | bytes accessed | tf_op | source)
XLA Modules:
  0.0 279.5 jit_solution(5447209523548036402)
XLA Ops:
  0.0 3.7 %copy.188 = f32[1,6,8,128,128]{4,1,3,2,0:T(8,128)S(1)} copy(f32[1,6,8,128,128]{4,3,2,1,0:T(8,128)} %param.11) | data formatting | bytes 6291456 | tf_op args[0]
  6.8 3.3 %collective-permute-start = (f32[6,1,128,128]{3,0,2,1:T(8,128)}, f32[6,1,128,128]{3,0,2,1:T(8,128)}, u32[]{:S(2)}, u32[]{:S(2)}) collective-permute-start(f32[6,1,128,128]{3,0,2,1:T(8,128)} %get-tuple-element.13), channel_id=1, source_target_pairs={{1,0},{2,1},{3,2},{4,3},{5,4},{6,5},{7,6},{8,7},{9,8},{10,9},{11,1... | collective-permute-start | bytes 1179656 | tf_op jit(solution)/shard_map/ppermute | solution.py:20
  10.1 3.5 %collective-permute-start.1 = (f32[6,1,128,128]{3,0,2,1:T(8,128)}, f32[6,1,128,128]{3,0,2,1:T(8,128)}, u32[]{:S(2)}, u32[]{:S(2)}) collective-permute-start(f32[6,1,128,128]{3,0,2,1:T(8,128)} %get-tuple-element.12), channel_id=1, source_target_pairs={{0,1},{1,2},{2,3},{3,4},{4,5},{5,6},{6,7},{7,8},{8,9},{9,10},{10,1... | collective-permute-start | bytes 1179656 | tf_op jit(solution)/shard_map/ppermute | solution.py:18
  14.3 10.4 %gather_fusion.2 = f32[1024,6,128]{2,1,0:T(8,128)} fusion(f32[6,1024,128]{2,0,1:T(8,128)} %bitcast.179, s32[1024]{0:T(1024)S(1)} %fusion.81), kind=kCustom, calls=%fused_computation.clone | custom fusion | bytes 6295552 | tf_op jit(solution)/shard_map/jit(_take)/gather | solution.py:31
  24.7 7.3 %bitcast_multiply_fusion.1 = f32[6,1024,128]{2,0,1:T(8,128)S(1)} fusion(f32[1024,6,128]{2,1,0:T(8,128)} %gather_fusion.2, f32[1024]{0:T(1024)S(1)} %broadcast_select_fusion, pred[1024]{0:T(1024)(128)(4,1)S(1)} %compare_and_fusion), kind=kLoop, calls=%fused_computation.32 | loop fusion | flops 1572864 | bytes 6296576 | tf_op jit(solution)/shard_map/mul | solution.py:34
  34.4 12.5 %all-to-all-start = ((f32[6,128,8,128]{3,2,0,1:T(8,128)}), f32[6,128,8,128]{3,2,0,1:T(8,128)}, u32[]{:S(2)}, u32[]{:S(2)}) async-start(f32[6,128,8,128]{3,2,0,1:T(8,128)} %copy.85), calls=%async_computation | async-start | bytes 6291456 | tf_op jit(solution)/shard_map/all_to_all | solution.py:35
  46.9 7.0 %fusion.94 = (f32[6,8,128,127]{3,0,2,1:T(8,128)}, f32[6,8,128,127]{3,0,2,1:T(8,128)S(1)}) fusion(f32[6,8,128,128]{3,0,2,1:T(8,128)} %bitcast.180), kind=kLoop, calls=%fused_computation.112 | loop fusion | bytes 12484608 | tf_op jit(solution)/shard_map/slice | solution.py:56
  53.9 5.2 %fusion.31 = f32[8,128,128,6]{2,3,1,0:T(8,128)} fusion(f32[6,8,128,128]{3,0,2,1:T(8,128)S(1)} %bitcast.184, f32[1,1,6,6]{3,0,2,1:T(1,128)S(1)} %get-tuple-element.20), kind=kOutput, calls=%fused_computation.53 | convolution fusion | flops 56180736 | bytes 7310336 | tf_op jit(solution)/shard_map/vu,vxyz->uxyz/dot_general | solution.py:43
  59.1 5.7 %fusion.23 = f32[8,128,128,6]{2,3,1,0:T(8,128)} fusion(f32[6,8,128,127]{3,0,2,1:T(8,128)S(1)} %get-tuple-element.15, f32[1,1,6,6]{3,0,2,1:T(1,128)S(1)} %get-tuple-element.23), kind=kOutput, calls=%fused_computation.45 | convolution fusion | flops 56623104 | bytes 6267024 | tf_op jit(solution)/shard_map/vu,vxyz->uxyz/dot_general | solution.py:43
  64.9 8.0 %fusion.33 = f32[8,128,128,6]{2,3,1,0:T(8,128)} fusion(f32[6,8,128,128]{3,0,2,1:T(8,128)} %bitcast.181, f32[1,1,6,6]{3,0,2,1:T(1,128)S(1)} %get-tuple-element.21), kind=kOutput, calls=%fused_computation.55 | convolution fusion | flops 56180736 | bytes 7307408 | tf_op jit(solution)/shard_map/vu,vxyz->uxyz/dot_general | solution.py:43
  72.9 7.4 %fusion.70 = f32[6,8,128,128]{3,0,2,1:T(8,128)} fusion(f32[1,6,8,128,128]{4,3,2,1,0:T(8,128)S(1)} %copy-done.4, f32[6,6]{1,0:T(8,128)S(1)} %reduce_sum.8), kind=kOutput, calls=%fused_computation.76 | convolution fusion | flops 56623140 | bytes 6291600 | tf_op jit(solution)/shard_map/vu,vxyz->uxyz/dot_general | solution.py:43
  80.3 5.3 %fusion.25 = f32[8,128,128,6]{2,3,1,0:T(8,128)} fusion(f32[6,8,128,127]{3,0,2,1:T(8,128)S(1)} %copy-done.6, f32[1,1,6,6]{3,0,2,1:T(1,128)S(1)} %get-tuple-element.19), kind=kOutput, calls=%fused_computation.47 | convolution fusion | flops 56623104 | bytes 6267024 | tf_op jit(solution)/shard_map/vu,vxyz->uxyz/dot_general | solution.py:43
  88.7 8.2 %fusion = f32[8,128,128,6]{2,3,1,0:T(8,128)} fusion(f32[6,1,128,128]{3,0,2,1:T(8,128)} %collective-permute-done, f32[6,8,128,128]{3,0,2,1:T(8,128)} %bitcast.183, f32[1,1,6,6]{3,0,2,1:T(1,128)S(1)} %get-tuple-element.22), kind=kOutput, calls=%fused_computation.6 | convolution fusion | flops 57507840 | bytes 6684816 | tf_op jit(solution)/shard_map/vu,vxyz->uxyz/dot_general | solution.py:43
  96.8 15.9 %bitcast_add_fusion.7 = f32[6,8,128,128]{3,0,2,1:T(8,128)} fusion(f32[1,6,8,128,128]{4,3,2,1,0:T(8,128)S(1)} %copy-done.5, f32[8,128,128,6]{2,3,1,0:T(8,128)} %fusion.23, f32[8,128,128,6]{2,3,1,0:T(8,128)} %fusion.25, f32[8,128,128,6]{2,3,1,0:T(8,128)} %fusion.31, f32[8,128,128,6]{2,3,1,0:T(8,128)} %fusion.33, f32[6,8,128,128]{3,0,2,1:T(8,128)} %fusion.70, ...), kind=kOutput, calls=%fused_computation.33 | convolution fusion | flops 63799296 | bytes 29229200 | tf_op jit(solution)/shard_map/vu,vxyz->uxyz/dot_general | solution.py:43
  112.8 3.2 %fusion.66 = f32[64,6,128]{2,0,1:T(8,128)S(1)} fusion(f32[6,128,8,128]{3,2,0,1:T(8,128)} %all-to-all-done, f32[64,6,128]{2,1,0:T(8,128)S(1)} %gather_fusion, s32[1024]{0:T(1024)S(1)} %eq.8), kind=kOutput, calls=%fused_computation.73 | convolution fusion | flops 604143616 | bytes 3543040 | tf_op jit(solution)/shard_map/sk,vkz->vsz/dot_general | solution.py:39
  116.1 6.8 %scatter_fusion = f32[6,1024,128]{2,0,1:T(8,128)} fusion(f32[6,1024,128]{2,0,1:T(8,128)} %bitcast.186, s32[64]{0:T(128)S(1)} %fusion.82, f32[64,6,128]{2,1,0:T(8,128)S(1)} %copy.89), kind=kCustom, calls=%fused_computation.4 | custom fusion | flops 49152 | bytes 590080 | tf_op jit(solution)/shard_map/scatter-add | solution.py:61
  129.1 5.4 %fusion.27 = f32[8,128,128,6]{2,3,1,0:T(8,128)} fusion(f32[6,8,128,128]{3,0,2,1:T(8,128)S(1)} %fusion.69, f32[1,1,6,6]{3,0,2,1:T(1,128)S(1)} %get-tuple-element.20), kind=kOutput, calls=%fused_computation.49 | convolution fusion | flops 56180736 | bytes 7310336 | tf_op jit(solution)/shard_map/vu,vxyz->uxyz/dot_general | solution.py:43
  134.5 5.1 %fusion.29 = f32[8,128,128,6]{2,3,1,0:T(8,128)} fusion(f32[6,8,128,128]{3,0,2,1:T(8,128)S(1)} %fusion.69, f32[1,1,6,6]{3,0,2,1:T(1,128)S(1)} %get-tuple-element.21), kind=kOutput, calls=%fused_computation.51 | convolution fusion | flops 56180736 | bytes 7310336 | tf_op jit(solution)/shard_map/vu,vxyz->uxyz/dot_general | solution.py:43
  139.6 5.8 %fusion.76 = f32[6,8,128,128]{3,0,2,1:T(8,128)} fusion(f32[6,8,128,128]{3,0,2,1:T(8,128)S(1)} %fusion.69, f32[6,6]{1,0:T(8,128)S(1)} %reduce_sum.8), kind=kOutput, calls=%fused_computation.90 | convolution fusion | flops 56623140 | bytes 6291600 | tf_op jit(solution)/shard_map/vu,vxyz->uxyz/dot_general | solution.py:43
  145.4 2.8 %collective-permute-start.2 = (f32[6,1,128,128]{3,0,2,1:T(8,128)S(1)}, f32[6,1,128,128]{3,0,2,1:T(8,128)S(1)}, u32[]{:S(2)}, u32[]{:S(2)}) collective-permute-start(f32[6,1,128,128]{3,0,2,1:T(8,128)S(1)} %get-tuple-element.9), channel_id=1, source_target_pairs={{1,0},{2,1},{3,2},{4,3},{5,4},{6,5},{7,6},{8,7},{9,8},{10,9},{11,1... | collective-permute-start | bytes 1179656 | tf_op jit(solution)/shard_map/ppermute | solution.py:20
  148.2 5.3 %fusion.21 = f32[8,128,128,6]{2,3,1,0:T(8,128)} fusion(f32[6,8,128,127]{3,0,2,1:T(8,128)S(1)} %get-tuple-element.10, f32[1,1,6,6]{3,0,2,1:T(1,128)S(1)} %get-tuple-element.19), kind=kOutput, calls=%fused_computation.43 | convolution fusion | flops 56623104 | bytes 6267024 | tf_op jit(solution)/shard_map/vu,vxyz->uxyz/dot_general | solution.py:43
  156.3 5.9 %fusion.19 = f32[8,128,128,6]{2,3,1,0:T(8,128)} fusion(f32[6,8,128,127]{3,0,2,1:T(8,128)S(1)} %get-tuple-element.11, f32[1,1,6,6]{3,0,2,1:T(1,128)S(1)} %get-tuple-element.23), kind=kOutput, calls=%fused_computation.41 | convolution fusion | flops 56623104 | bytes 6267024 | tf_op jit(solution)/shard_map/vu,vxyz->uxyz/dot_general | solution.py:43
  162.3 5.8 %fusion.8 = f32[8,128,128,6]{2,3,1,0:T(8,128)} fusion(f32[6,1,128,128]{3,0,2,1:T(8,128)S(1)} %collective-permute-done.2, f32[6,8,128,128]{3,0,2,1:T(8,128)S(1)} %fusion.69, f32[1,1,6,6]{3,0,2,1:T(1,128)S(1)} %get-tuple-element.22), kind=kOutput, calls=%fused_computation.14 | convolution fusion | flops 57507840 | bytes 6684816 | tf_op jit(solution)/shard_map/vu,vxyz->uxyz/dot_general | solution.py:43
  168.1 14.1 %fusion.17 = f32[6,8,128,128]{3,0,2,1:T(8,128)} fusion(f32[8,128,128,6]{2,3,1,0:T(8,128)} %fusion.19, f32[8,128,128,6]{2,3,1,0:T(8,128)} %fusion.21, f32[8,128,128,6]{2,3,1,0:T(8,128)} %fusion.27, f32[8,128,128,6]{2,3,1,0:T(8,128)} %fusion.29, f32[6,8,128,128]{3,0,2,1:T(8,128)} %fusion.76, f32[8,128,128,6]{2,3,1,0:T(8,128)} %fusion.8, ...), kind=kOutput, calls=%fused_computation.26 | convolution fusion | flops 63799296 | bytes 29229200 | tf_op jit(solution)/shard_map/vu,vxyz->uxyz/dot_general | solution.py:43
  182.2 7.9 %bitcast_add_fusion.14 = (f32[6,1024,128]{2,0,1:T(8,128)}, f32[6,1024,128]{2,0,1:T(8,128)}) fusion(f32[1,6,8,128,128]{4,1,3,2,0:T(8,128)S(1)} %copy-done.3, f32[6,1024,128]{2,0,1:T(8,128)} %scatter_fusion, f32[6,8,128,128]{3,0,2,1:T(8,128)} %fusion.17), kind=kLoop, calls=%fused_computation.104 | loop fusion | flops 2359296 | bytes 15728640 | tf_op jit(solution)/shard_map/add | solution.py:89
  190.1 10.4 %gather_fusion.3 = f32[1024,6,128]{2,1,0:T(8,128)} fusion(f32[6,1024,128]{2,0,1:T(8,128)} %get-tuple-element.6, s32[1024]{0:T(1024)S(1)} %fusion.81), kind=kCustom, calls=%fused_computation.1.clone | custom fusion | bytes 6295552 | tf_op jit(solution)/shard_map/jit(_take)/gather | solution.py:31
  200.5 7.3 %bitcast_multiply_fusion = f32[6,1024,128]{2,0,1:T(8,128)S(1)} fusion(f32[1024,6,128]{2,1,0:T(8,128)} %gather_fusion.3, f32[1024]{0:T(1024)S(1)} %broadcast_select_fusion, pred[1024]{0:T(1024)(128)(4,1)S(1)} %compare_and_fusion), kind=kLoop, calls=%fused_computation.22 | loop fusion | flops 1572864 | bytes 6296576 | tf_op jit(solution)/shard_map/mul | solution.py:34
  210.3 12.4 %all-to-all-start.1 = ((f32[6,128,8,128]{3,2,0,1:T(8,128)}), f32[6,128,8,128]{3,2,0,1:T(8,128)}, u32[]{:S(2)}, u32[]{:S(2)}) async-start(f32[6,128,8,128]{3,2,0,1:T(8,128)} %copy.97), calls=%async_computation.1 | async-start | bytes 6291456 | tf_op jit(solution)/shard_map/all_to_all | solution.py:35
  222.6 2.8 gather_fusion.1
  225.4 38.6 %all-to-all-done.1 = f32[6,128,8,128]{3,2,0,1:T(8,128)} async-done(((f32[6,128,8,128]{3,2,0,1:T(8,128)}), f32[6,128,8,128]{3,2,0,1:T(8,128)}, u32[]{:S(2)}, u32[]{:S(2)}) %all-to-all-start.1) | async-done | bytes 3145760 | tf_op jit(solution)/shard_map/all_to_all | solution.py:35
  264.0 3.2 %fusion.57 = f32[64,6,128]{2,0,1:T(8,128)S(1)} fusion(f32[6,128,8,128]{3,2,0,1:T(8,128)} %all-to-all-done.1, f32[64,6,128]{2,1,0:T(8,128)S(1)} %gather_fusion.1, s32[1024]{0:T(1024)S(1)} %eq.8), kind=kOutput, calls=%fused_computation.70 | convolution fusion | flops 604143616 | bytes 3543040 | tf_op jit(solution)/shard_map/sk,vkz->vsz/dot_general | solution.py:39
  267.3 6.8 %scatter_fusion.1 = f32[6,1024,128]{2,0,1:T(8,128)} fusion(f32[6,1024,128]{2,0,1:T(8,128)} %get-tuple-element.7, s32[64]{0:T(128)S(1)} %fusion.82, f32[64,6,128]{2,1,0:T(8,128)S(1)} %copy.100), kind=kCustom, calls=%fused_computation.5 | custom fusion | flops 49152 | bytes 590080 | tf_op jit(solution)/shard_map/scatter-add | solution.py:61
  (63 shorter events, 25.9 us)
Async XLA Ops:
  0.0 13.6 %copy-start.10 = (s32[1,128,8]{1,2,0:T(8,128)S(1)}, s32[1,128,8]{1,2,0:T(8,128)}, u32[]{:S(2)}) copy-start(s32[1,128,8]{1,2,0:T(8,128)} %param.15) | copy-start | bytes 12292
  0.0 13.9 %copy-start.11 = (f32[1,128,8]{1,2,0:T(8,128)S(1)}, f32[1,128,8]{1,2,0:T(8,128)}, u32[]{:S(2)}) copy-start(f32[1,128,8]{1,2,0:T(8,128)} %param.17) | copy-start | bytes 12292
  0.0 14.1 %copy-start.13 = (s32[1,128]{1,0:T(1,128)S(1)}, s32[1,128]{1,0:T(1,128)}, u32[]{:S(2)}) copy-start(s32[1,128]{1,0:T(1,128)} %param.16) | copy-start | bytes 1540
  3.7 1.9 copy-start
  6.8 81.8 %collective-permute-start = (f32[6,1,128,128]{3,0,2,1:T(8,128)}, f32[6,1,128,128]{3,0,2,1:T(8,128)}, u32[]{:S(2)}, u32[]{:S(2)}) collective-permute-start(f32[6,1,128,128]{3,0,2,1:T(8,128)} %get-tuple-element.13), channel_id=1, source_target_pairs={{1,0},{2,1},{3,2},{4,3},{5,4},{6,5},{7,6},{8,7},{9,8},{10,9},{11,1... | collective-permute-start | bytes 1179656 | tf_op jit(solution)/shard_map/ppermute | solution.py:20
  10.1 86.7 %collective-permute-start.1 = (f32[6,1,128,128]{3,0,2,1:T(8,128)}, f32[6,1,128,128]{3,0,2,1:T(8,128)}, u32[]{:S(2)}, u32[]{:S(2)}) collective-permute-start(f32[6,1,128,128]{3,0,2,1:T(8,128)} %get-tuple-element.12), channel_id=1, source_target_pairs={{0,1},{1,2},{2,3},{3,4},{4,5},{5,6},{6,7},{7,8},{8,9},{9,10},{10,1... | collective-permute-start | bytes 1179656 | tf_op jit(solution)/shard_map/ppermute | solution.py:18
  34.4 78.4 %all-to-all-start = ((f32[6,128,8,128]{3,2,0,1:T(8,128)}), f32[6,128,8,128]{3,2,0,1:T(8,128)}, u32[]{:S(2)}, u32[]{:S(2)}) async-start(f32[6,128,8,128]{3,2,0,1:T(8,128)} %copy.85), calls=%async_computation | async-start | bytes 6291456 | tf_op jit(solution)/shard_map/all_to_all | solution.py:35
  46.9 7.0 %copy-start.9 = (f32[1,6,6,6]{3,0,2,1:T(1,128)S(1)}, f32[1,6,6,6]{3,0,2,1:T(1,128)}, u32[]{:S(2)}) copy-start(f32[1,6,6,6]{3,0,2,1:T(1,128)} %param.14) | copy-start | bytes 2596
  46.9 7.0 %copy-start.1 = (f32[1,6,8,128,128]{4,1,3,2,0:T(8,128)S(1)}, f32[1,6,8,128,128]{4,1,3,2,0:T(8,128)}, u32[]{:S(2)}) copy-start(f32[1,6,8,128,128]{4,1,3,2,0:T(8,128)} %copy-done) | copy-start | bytes 9437188
  59.1 5.7 %copy-start.14 = (s32[1,64]{1,0:T(1,128)S(1)}, s32[1,64]{1,0:T(1,128)}, u32[]{:S(2)}) copy-start(s32[1,64]{1,0:T(1,128)} %param.19) | copy-start | bytes 772
  64.8 8.0 %copy-start.4 = (f32[1,6,8,128,128]{4,3,2,1,0:T(8,128)S(1)}, f32[1,6,8,128,128]{4,3,2,1,0:T(8,128)}, u32[]{:S(2)}) copy-start(f32[1,6,8,128,128]{4,3,2,1,0:T(8,128)} %param.11) | copy-start | bytes 9437188
  72.9 7.4 %copy-start.6 = (f32[6,8,128,127]{3,0,2,1:T(8,128)S(1)}, f32[6,8,128,127]{3,0,2,1:T(8,128)}, u32[]{:S(2)}) copy-start(f32[6,8,128,127]{3,0,2,1:T(8,128)} %get-tuple-element.14) | copy-start | bytes 9363460
  80.3 8.1 %copy-start.12 = (s32[1,128,8]{1,2,0:T(8,128)S(1)}, s32[1,128,8]{1,2,0:T(8,128)}, u32[]{:S(2)}) copy-start(s32[1,128,8]{1,2,0:T(8,128)} %param.18) | copy-start | bytes 12292
  88.6 8.2 %copy-start.2 = (f32[1,6,8,128,128]{4,1,3,2,0:T(8,128)S(1)}, f32[1,6,8,128,128]{4,1,3,2,0:T(8,128)}, u32[]{:S(2)}) copy-start(f32[1,6,8,128,128]{4,1,3,2,0:T(8,128)} %copy-done) | copy-start | bytes 9437188
  88.6 8.2 %copy-start.5 = (f32[1,6,8,128,128]{4,3,2,1,0:T(8,128)S(1)}, f32[1,6,8,128,128]{4,3,2,1,0:T(8,128)}, u32[]{:S(2)}) copy-start(f32[1,6,8,128,128]{4,3,2,1,0:T(8,128)} %param.12) | copy-start | bytes 9437188
  88.6 8.2 %copy-start.7 = (f32[1,8,128,128]{3,2,1,0:T(8,128)S(1)}, f32[1,8,128,128]{3,2,1,0:T(8,128)}, u32[]{:S(2)}) copy-start(f32[1,8,128,128]{3,2,1,0:T(8,128)} %param.13) | copy-start | bytes 1572868
  145.4 16.9 %collective-permute-start.2 = (f32[6,1,128,128]{3,0,2,1:T(8,128)S(1)}, f32[6,1,128,128]{3,0,2,1:T(8,128)S(1)}, u32[]{:S(2)}, u32[]{:S(2)}) collective-permute-start(f32[6,1,128,128]{3,0,2,1:T(8,128)S(1)} %get-tuple-element.9), channel_id=1, source_target_pairs={{1,0},{2,1},{3,2},{4,3},{5,4},{6,5},{7,6},{8,7},{9,8},{10,9},{11,1... | collective-permute-start | bytes 1179656 | tf_op jit(solution)/shard_map/ppermute | solution.py:20
  153.6 14.5 %collective-permute-start.3 = (f32[6,1,128,128]{3,0,2,1:T(8,128)S(1)}, f32[6,1,128,128]{3,0,2,1:T(8,128)S(1)}, u32[]{:S(2)}, u32[]{:S(2)}) collective-permute-start(f32[6,1,128,128]{3,0,2,1:T(8,128)S(1)} %get-tuple-element.8), channel_id=1, source_target_pairs={{0,1},{1,2},{2,3},{3,4},{4,5},{5,6},{6,7},{7,8},{8,9},{9,10},{10,1... | collective-permute-start | bytes 1179656 | tf_op jit(solution)/shard_map/ppermute | solution.py:18
  162.3 5.8 %copy-start.8 = (f32[1,8,128,128]{3,2,1,0:T(8,128)S(1)}, f32[1,8,128,128]{3,2,1,0:T(8,128)}, u32[]{:S(2)}) copy-start(f32[1,8,128,128]{3,2,1,0:T(8,128)} %param.13) | copy-start | bytes 1572868
  168.1 14.1 %copy-start.3 = (f32[1,6,8,128,128]{4,1,3,2,0:T(8,128)S(1)}, f32[1,6,8,128,128]{4,1,3,2,0:T(8,128)}, u32[]{:S(2)}) copy-start(f32[1,6,8,128,128]{4,1,3,2,0:T(8,128)} %copy-done) | copy-start | bytes 9437188
  210.3 53.7 %all-to-all-start.1 = ((f32[6,128,8,128]{3,2,0,1:T(8,128)}), f32[6,128,8,128]{3,2,0,1:T(8,128)}, u32[]{:S(2)}, u32[]{:S(2)}) async-start(f32[6,128,8,128]{3,2,0,1:T(8,128)} %copy.97), calls=%async_computation.1 | async-start | bytes 6291456 | tf_op jit(solution)/shard_map/all_to_all | solution.py:35
where the time goes:
time: 284 us; the launch traced here: 279 us
  matrix products  110 us (39%)
  local copies, waits for them, and re-layouts  47.3 us (17%)
  other arithmetic  46.2 us (16%)
  waiting for transfers between devices  38.6 us (14%)
  starting transfers between devices  37.3 us (13%)
    dot_general x14, matrix products, apply_block(): jnp.einsum('vu,vxyz->uxyz', matrix, values, precision=lax.Precision.HIGHEST)  103 us
    all_to_all x2, waiting for transfers between devices, fringe_values(): lax.all_to_all(outgoing, ('comp', 'blk'), split_axis=1, concat_axis=1, ti...  38.6 us
    all_to_all x2, starting transfers between devices, fringe_values(): lax.all_to_all(outgoing, ('comp', 'blk'), split_axis=1, concat_axis=1, ti...  24.9 us
    gather x2, local copies, waits for them, and re-layouts, fringe_values(): picked = jnp.take(flat, send_tile.reshape(-1), axis=1)  20.8 us
    mul x2, other arithmetic, fringe_values(): picked * scale[None, :, None]  14.6 us
    scatter-add x2, other arithmetic, residual_of(): rate_flat.at[:, rows, :].add(PENALTY * (interp - field_flat[:, rows, :]))  13.6 us
    add x2, other arithmetic, shards(): middle = start + TIME_STEP * first  10 us
    slice x2, local copies, waits for them, and re-layouts, residual_of(): field[:, :, :, 1:]  8.32 us
  transfers between devices with their start and end apart: 6, of which 1 were waited for; matrix products, arithmetic and copies ran while one was open for 38% of the time, Pallas kernels for 0%

commit v1 on v0

--- a/solution.py
+++ b/solution.py
@@ -32,7 +32,15 @@
     live = lax.broadcasted_iota(jnp.int32, (peers, capacity), 1) < send_count.reshape(peers, 1)
     scale = jnp.where(live, send_weight, 0.0).reshape(-1)
     outgoing = (picked * scale[None, :, None]).reshape(nvar, peers, capacity, length)
-    arrived = lax.all_to_all(outgoing, ("comp", "blk"), split_axis=1, concat_axis=1, tiled=True)
+    arrived = jnp.concatenate(
+        lax.all_to_all(
+            jnp.stack(jnp.split(outgoing, lax.axis_size(("comp", "blk")), axis=1)),
+            ("comp", "blk"),
+            0,
+            0,
+        ),
+        axis=1,
+    )
     arrived = arrived.reshape(nvar, peers * capacity, length)
     slot_ids = lax.broadcasted_iota(jnp.int32, (count_slots, 1), 0)
     onehot = (recv_slot.reshape(1, -1) == slot_ids).astype(jnp.float32)

time: 284 us -> 442 us (1.56)
  local copies, waits for them, and re-layouts: 47.3 us -> 202 us
    unnamed x34 -> x284, local copies, waits for them, and re-layouts: 6.03 us -> 162 us
    reshape x2 -> x0, local copies, waits for them, and re-layouts: 4.84 us -> none  [fringe_values(): (picked * scale[None, :, None]).reshape(nvar, peers, capacity, length)]
  transfers between devices with their start and end apart: 6 -> 6, of which waited for: 1 -> 1; matrix products, arithmetic and copies ran while one was open for 38% -> 20% of each run, Pallas kernels for 0% -> 0%
where the time goes in v1:
time: 442 us; the launch traced here: 435 us
  local copies, waits for them, and re-layouts  202 us (46%)
  matrix products  110 us (25%)
  other arithmetic  46.4 us (10%)
  waiting for transfers between devices  38.8 us (9%)
  starting transfers between devices  37.4 us (8%)
    unnamed x284, local copies, waits for them, and re-layouts  162 us
    dot_general x14, matrix products, apply_block(): jnp.einsum('vu,vxyz->uxyz', matrix, values, precision=lax.Precision.HIGHEST)  104 us
    all_to_all x2, waiting for transfers between devices, fringe_values(): lax.all_to_all(jnp.stack(jnp.split(outgoing, lax.axis_size(('comp', 'blk'...  38.8 us
    all_to_all x2, starting transfers between devices, fringe_values(): lax.all_to_all(jnp.stack(jnp.split(outgoing, lax.axis_size(('comp', 'blk'...  26 us
    gather x2, local copies, waits for them, and re-layouts, fringe_values(): picked = jnp.take(flat, send_tile.reshape(-1), axis=1)  20.8 us
    mul x2, other arithmetic, fringe_values(): picked * scale[None, :, None]  14.9 us
    scatter-add x2, other arithmetic, residual_of(): rate_flat.at[:, rows, :].add(PENALTY * (interp - field_flat[:, rows, :]))  13.5 us
    add x2, other arithmetic, shards(): middle = start + TIME_STEP * first  10.1 us
  transfers between devices with their start and end apart: 6, of which 1 were waited for; matrix products, arithmetic and copies ran while one was open for 20% of the time, Pallas kernels for 0%

profile of v1, /device:TPU:1, one launch (start us, length us, event | category | flops | bytes accessed | tf_op | source)
XLA Modules:
  0.0 435.3 jit_solution(7182401021654842179)
XLA Ops:
  0.9 5.7 %copy.1974 = f32[1,6,8,128,128]{4,1,3,2,0:T(8,128)} copy(f32[1,6,8,128,128]{4,3,2,1,0:T(8,128)} %param.11) | data formatting | bytes 6291456 | tf_op args[0]
  7.0 10.4 %gather_fusion.2 = f32[1024,6,128]{2,1,0:T(8,128)} fusion(f32[6,1024,128]{2,0,1:T(8,128)} %bitcast.1210, s32[1024]{0:T(1024)S(1)} %fusion.81), kind=kCustom, calls=%fused_computation.clone | custom fusion | bytes 6295552 | tf_op jit(solution)/shard_map/jit(_take)/gather | solution.py:31
  17.4 7.3 %bitcast_multiply_fusion.1 = f32[6,1024,128]{2,0,1:T(8,128)S(1)} fusion(f32[1024,6,128]{2,1,0:T(8,128)} %gather_fusion.2, f32[1024]{0:T(1024)S(1)} %broadcast_select_fusion, pred[1024]{0:T(1024)(128)(4,1)S(1)} %compare_and_fusion), kind=kLoop, calls=%fused_computation.32 | loop fusion | flops 1572864 | bytes 6296576 | tf_op jit(solution)/shard_map/mul | solution.py:34
  103.6 11.9 %all-to-all-start = ((f32[128,6,1,8,128]{4,3,1,2,0:T(8,128)}), f32[128,6,1,8,128]{4,3,1,2,0:T(8,128)}, u32[]{:S(2)}, u32[]{:S(2)}) async-start(f32[128,6,1,8,128]{4,3,1,2,0:T(8,128)} %constant_dynamic-update-slice_fusion), calls=%async_computation | async-start | bytes 6291456 | tf_op jit(solution)/shard_map/all_to_all | solution.py:36
  117.8 3.0 collective-permute-start
  120.9 2.8 collective-permute-start.1
  123.7 6.9 %fusion.108 = (f32[6,8,128,127]{3,0,2,1:T(8,128)}, f32[6,8,128,127]{3,0,2,1:T(8,128)S(1)}) fusion(f32[6,8,128,128]{3,0,2,1:T(8,128)} %bitcast.1212), kind=kLoop, calls=%fused_computation.638 | loop fusion | bytes 12484608 | tf_op jit(solution)/shard_map/slice | solution.py:64
  130.6 5.5 %fusion.31 = f32[8,128,128,6]{2,3,1,0:T(8,128)} fusion(f32[6,8,128,128]{3,0,2,1:T(8,128)S(1)} %bitcast.1216, f32[1,1,6,6]{3,0,2,1:T(1,128)S(1)} %get-tuple-element.276), kind=kOutput, calls=%fused_computation.53 | convolution fusion | flops 56180736 | bytes 7310336 | tf_op jit(solution)/shard_map/vu,vxyz->uxyz/dot_general | solution.py:51
  136.0 5.7 %fusion.23 = f32[8,128,128,6]{2,3,1,0:T(8,128)} fusion(f32[6,8,128,127]{3,0,2,1:T(8,128)S(1)} %get-tuple-element.271, f32[1,1,6,6]{3,0,2,1:T(1,128)S(1)} %get-tuple-element.279), kind=kOutput, calls=%fused_computation.45 | convolution fusion | flops 56623104 | bytes 6267024 | tf_op jit(solution)/shard_map/vu,vxyz->uxyz/dot_general | solution.py:51
  141.8 8.0 %fusion.33 = f32[8,128,128,6]{2,3,1,0:T(8,128)} fusion(f32[6,8,128,128]{3,0,2,1:T(8,128)} %bitcast.1213, f32[1,1,6,6]{3,0,2,1:T(1,128)S(1)} %get-tuple-element.277), kind=kOutput, calls=%fused_computation.55 | convolution fusion | flops 56180736 | bytes 7307408 | tf_op jit(solution)/shard_map/vu,vxyz->uxyz/dot_general | solution.py:51
  149.8 7.2 %fusion.70 = f32[6,8,128,128]{3,0,2,1:T(8,128)} fusion(f32[1,6,8,128,128]{4,3,2,1,0:T(8,128)S(1)} %copy-done.3, f32[6,6]{1,0:T(8,128)S(1)} %reduce_sum.8), kind=kOutput, calls=%fused_computation.332 | convolution fusion | flops 56623140 | bytes 6291600 | tf_op jit(solution)/shard_map/vu,vxyz->uxyz/dot_general | solution.py:51
  157.1 5.8 %fusion.25 = f32[8,128,128,6]{2,3,1,0:T(8,128)} fusion(f32[6,8,128,127]{3,0,2,1:T(8,128)S(1)} %copy-done.5, f32[1,1,6,6]{3,0,2,1:T(1,128)S(1)} %get-tuple-element.275), kind=kOutput, calls=%fused_computation.47 | convolution fusion | flops 56623104 | bytes 6267024 | tf_op jit(solution)/shard_map/vu,vxyz->uxyz/dot_general | solution.py:51
  165.9 8.2 %fusion = f32[8,128,128,6]{2,3,1,0:T(8,128)} fusion(f32[6,1,128,128]{3,0,2,1:T(8,128)} %collective-permute-done, f32[6,8,128,128]{3,0,2,1:T(8,128)} %bitcast.1215, f32[1,1,6,6]{3,0,2,1:T(1,128)S(1)} %get-tuple-element.278), kind=kOutput, calls=%fused_computation.6 | convolution fusion | flops 57507840 | bytes 6684816 | tf_op jit(solution)/shard_map/vu,vxyz->uxyz/dot_general | solution.py:51
  174.1 15.7 %bitcast_add_fusion.7 = f32[6,8,128,128]{3,0,2,1:T(8,128)} fusion(f32[1,6,8,128,128]{4,3,2,1,0:T(8,128)S(1)} %copy-done.4, f32[8,128,128,6]{2,3,1,0:T(8,128)} %fusion.23, f32[8,128,128,6]{2,3,1,0:T(8,128)} %fusion.25, f32[8,128,128,6]{2,3,1,0:T(8,128)} %fusion.31, f32[8,128,128,6]{2,3,1,0:T(8,128)} %fusion.33, f32[6,8,128,128]{3,0,2,1:T(8,128)} %fusion.70, ...), kind=kOutput, calls=%fused_computation.33 | convolution fusion | flops 63799296 | bytes 29229200 | tf_op jit(solution)/shard_map/vu,vxyz->uxyz/dot_general | solution.py:51
  189.9 3.2 fusion.66
  193.2 6.7 %scatter_fusion = f32[6,1024,128]{2,0,1:T(8,128)} fusion(f32[6,1024,128]{2,0,1:T(8,128)} %bitcast.1218, s32[64]{0:T(128)S(1)} %fusion.82, f32[64,6,128]{2,1,0:T(8,128)S(1)} %copy.724), kind=kCustom, calls=%fused_computation.4 | custom fusion | flops 49152 | bytes 590080 | tf_op jit(solution)/shard_map/scatter-add | solution.py:69
  206.1 5.2 %fusion.27 = f32[8,128,128,6]{2,3,1,0:T(8,128)} fusion(f32[6,8,128,128]{3,0,2,1:T(8,128)S(1)} %fusion.69, f32[1,1,6,6]{3,0,2,1:T(1,128)S(1)} %get-tuple-element.276), kind=kOutput, calls=%fused_computation.49 | convolution fusion | flops 56180736 | bytes 7310336 | tf_op jit(solution)/shard_map/vu,vxyz->uxyz/dot_general | solution.py:51
  211.3 5.2 %fusion.29 = f32[8,128,128,6]{2,3,1,0:T(8,128)} fusion(f32[6,8,128,128]{3,0,2,1:T(8,128)S(1)} %fusion.69, f32[1,1,6,6]{3,0,2,1:T(1,128)S(1)} %get-tuple-element.277), kind=kOutput, calls=%fused_computation.51 | convolution fusion | flops 56180736 | bytes 7310336 | tf_op jit(solution)/shard_map/vu,vxyz->uxyz/dot_general | solution.py:51
  216.5 5.8 %fusion.76 = f32[6,8,128,128]{3,0,2,1:T(8,128)} fusion(f32[6,8,128,128]{3,0,2,1:T(8,128)S(1)} %fusion.69, f32[6,6]{1,0:T(8,128)S(1)} %reduce_sum.8), kind=kOutput, calls=%fused_computation.602 | convolution fusion | flops 56623140 | bytes 6291600 | tf_op jit(solution)/shard_map/vu,vxyz->uxyz/dot_general | solution.py:51
  224.9 5.4 %fusion.21 = f32[8,128,128,6]{2,3,1,0:T(8,128)} fusion(f32[6,8,128,127]{3,0,2,1:T(8,128)S(1)} %get-tuple-element.138, f32[1,1,6,6]{3,0,2,1:T(1,128)S(1)} %get-tuple-element.275), kind=kOutput, calls=%fused_computation.43 | convolution fusion | flops 56623104 | bytes 6267024 | tf_op jit(solution)/shard_map/vu,vxyz->uxyz/dot_general | solution.py:51
  230.3 2.9 collective-permute-start.3
  233.2 5.9 %fusion.19 = f32[8,128,128,6]{2,3,1,0:T(8,128)} fusion(f32[6,8,128,127]{3,0,2,1:T(8,128)S(1)} %get-tuple-element.139, f32[1,1,6,6]{3,0,2,1:T(1,128)S(1)} %get-tuple-element.279), kind=kOutput, calls=%fused_computation.41 | convolution fusion | flops 56623104 | bytes 6267024 | tf_op jit(solution)/shard_map/vu,vxyz->uxyz/dot_general | solution.py:51
  239.2 5.9 %fusion.8 = f32[8,128,128,6]{2,3,1,0:T(8,128)} fusion(f32[6,1,128,128]{3,0,2,1:T(8,128)S(1)} %collective-permute-done.2, f32[6,8,128,128]{3,0,2,1:T(8,128)S(1)} %fusion.69, f32[1,1,6,6]{3,0,2,1:T(1,128)S(1)} %get-tuple-element.278), kind=kOutput, calls=%fused_computation.14 | convolution fusion | flops 57507840 | bytes 6684816 | tf_op jit(solution)/shard_map/vu,vxyz->uxyz/dot_general | solution.py:51
  245.0 14.1 %fusion.17 = f32[6,8,128,128]{3,0,2,1:T(8,128)} fusion(f32[8,128,128,6]{2,3,1,0:T(8,128)} %fusion.19, f32[8,128,128,6]{2,3,1,0:T(8,128)} %fusion.21, f32[8,128,128,6]{2,3,1,0:T(8,128)} %fusion.27, f32[8,128,128,6]{2,3,1,0:T(8,128)} %fusion.29, f32[6,8,128,128]{3,0,2,1:T(8,128)} %fusion.76, f32[8,128,128,6]{2,3,1,0:T(8,128)} %fusion.8, ...), kind=kOutput, calls=%fused_computation.26 | convolution fusion | flops 63799296 | bytes 29229200 | tf_op jit(solution)/shard_map/vu,vxyz->uxyz/dot_general | solution.py:51
  259.1 8.0 %bitcast_add_fusion.14 = (f32[6,1024,128]{2,0,1:T(8,128)}, f32[6,1024,128]{2,0,1:T(8,128)}) fusion(f32[1,6,8,128,128]{4,1,3,2,0:T(8,128)S(1)} %copy-done.2, f32[6,1024,128]{2,0,1:T(8,128)} %scatter_fusion, f32[6,8,128,128]{3,0,2,1:T(8,128)} %fusion.17), kind=kLoop, calls=%fused_computation.616 | loop fusion | flops 2359296 | bytes 15728640 | tf_op jit(solution)/shard_map/add | solution.py:97
  267.1 10.4 %gather_fusion.3 = f32[1024,6,128]{2,1,0:T(8,128)} fusion(f32[6,1024,128]{2,0,1:T(8,128)} %get-tuple-element.134, s32[1024]{0:T(1024)S(1)} %fusion.81), kind=kCustom, calls=%fused_computation.1.clone | custom fusion | bytes 6295552 | tf_op jit(solution)/shard_map/jit(_take)/gather | solution.py:31
  277.5 7.6 %bitcast_multiply_fusion = f32[6,1024,128]{2,0,1:T(8,128)S(1)} fusion(f32[1024,6,128]{2,1,0:T(8,128)} %gather_fusion.3, f32[1024]{0:T(1024)S(1)} %broadcast_select_fusion, pred[1024]{0:T(1024)(128)(4,1)S(1)} %compare_and_fusion), kind=kLoop, calls=%fused_computation.22 | loop fusion | flops 1572864 | bytes 6296576 | tf_op jit(solution)/shard_map/mul | solution.py:34
  364.1 14.1 %all-to-all-start.1 = ((f32[128,6,1,8,128]{4,3,1,2,0:T(8,128)}), f32[128,6,1,8,128]{4,3,1,2,0:T(8,128)}, u32[]{:S(2)}, u32[]{:S(2)}) async-start(f32[128,6,1,8,128]{4,3,1,2,0:T(8,128)} %constant_dynamic-update-slice_fusion.128), calls=%async_computation.1 | async-start | bytes 6291456 | tf_op jit(solution)/shard_map/all_to_all | solution.py:36
  378.2 2.8 gather_fusion.1
  381.0 38.8 %all-to-all-done.1 = f32[128,6,1,8,128]{4,3,1,2,0:T(8,128)} async-done(((f32[128,6,1,8,128]{4,3,1,2,0:T(8,128)}), f32[128,6,1,8,128]{4,3,1,2,0:T(8,128)}, u32[]{:S(2)}, u32[]{:S(2)}) %all-to-all-start.1) | async-done | bytes 3145760 | tf_op jit(solution)/shard_map/all_to_all | solution.py:36
  419.7 3.2 fusion.57
  423.0 6.8 %scatter_fusion.1 = f32[6,1024,128]{2,0,1:T(8,128)} fusion(f32[6,1024,128]{2,0,1:T(8,128)} %get-tuple-element.135, s32[64]{0:T(128)S(1)} %fusion.82, f32[64,6,128]{2,1,0:T(8,128)S(1)} %copy.862), kind=kCustom, calls=%fused_computation.5 | custom fusion | flops 49152 | bytes 590080 | tf_op jit(solution)/shard_map/scatter-add | solution.py:69
  (327 shorter events, 178.5 us)
Async XLA Ops:
  0.9 5.7 %copy-start.9 = (f32[1,128,8]{1,2,0:T(8,128)S(1)}, f32[1,128,8]{1,2,0:T(8,128)}, u32[]{:S(2)}) copy-start(f32[1,128,8]{1,2,0:T(8,128)} %param.17) | copy-start | bytes 12292
  0.9 5.9 %copy-start.11 = (s32[1,128]{1,0:T(1,128)S(1)}, s32[1,128]{1,0:T(1,128)}, u32[]{:S(2)}) copy-start(s32[1,128]{1,0:T(1,128)} %param.16) | copy-start | bytes 1540
  103.6 86.2 %all-to-all-start = ((f32[128,6,1,8,128]{4,3,1,2,0:T(8,128)}), f32[128,6,1,8,128]{4,3,1,2,0:T(8,128)}, u32[]{:S(2)}, u32[]{:S(2)}) async-start(f32[128,6,1,8,128]{4,3,1,2,0:T(8,128)} %constant_dynamic-update-slice_fusion), calls=%async_computation | async-start | bytes 6291456 | tf_op jit(solution)/shard_map/all_to_all | solution.py:36
  117.8 48.1 %collective-permute-start = (f32[6,1,128,128]{3,0,2,1:T(8,128)}, f32[6,1,128,128]{3,0,2,1:T(8,128)}, u32[]{:S(2)}, u32[]{:S(2)}) collective-permute-start(f32[6,1,128,128]{3,0,2,1:T(8,128)} %get-tuple-element.269), channel_id=1, source_target_pairs={{1,0},{2,1},{3,2},{4,3},{5,4},{6,5},{7,6},{8,7},{9,8},{10,9},{11,1... | collective-permute-start | bytes 1179656 | tf_op jit(solution)/shard_map/ppermute | solution.py:20
  120.9 9.7 %copy-start.8 = (f32[1,6,6,6]{3,0,2,1:T(1,128)S(1)}, f32[1,6,6,6]{3,0,2,1:T(1,128)}, u32[]{:S(2)}) copy-start(f32[1,6,6,6]{3,0,2,1:T(1,128)} %param.14) | copy-start | bytes 2596
  120.9 9.7 %copy-start = (f32[1,6,8,128,128]{4,1,3,2,0:T(8,128)S(1)}, f32[1,6,8,128,128]{4,1,3,2,0:T(8,128)}, u32[]{:S(2)}) copy-start(f32[1,6,8,128,128]{4,1,3,2,0:T(8,128)} %copy.1974) | copy-start | bytes 9437188
  120.9 53.2 %collective-permute-start.1 = (f32[6,1,128,128]{3,0,2,1:T(8,128)}, f32[6,1,128,128]{3,0,2,1:T(8,128)}, u32[]{:S(2)}, u32[]{:S(2)}) collective-permute-start(f32[6,1,128,128]{3,0,2,1:T(8,128)} %get-tuple-element.268), channel_id=1, source_target_pairs={{0,1},{1,2},{2,3},{3,4},{4,5},{5,6},{6,7},{7,8},{8,9},{9,10},{10,1... | collective-permute-start | bytes 1179656 | tf_op jit(solution)/shard_map/ppermute | solution.py:18
  136.0 5.8 %copy-start.12 = (s32[1,64]{1,0:T(1,128)S(1)}, s32[1,64]{1,0:T(1,128)}, u32[]{:S(2)}) copy-start(s32[1,64]{1,0:T(1,128)} %param.19) | copy-start | bytes 772
  141.8 8.0 %copy-start.3 = (f32[1,6,8,128,128]{4,3,2,1,0:T(8,128)S(1)}, f32[1,6,8,128,128]{4,3,2,1,0:T(8,128)}, u32[]{:S(2)}) copy-start(f32[1,6,8,128,128]{4,3,2,1,0:T(8,128)} %param.11) | copy-start | bytes 9437188
  149.8 7.2 %copy-start.5 = (f32[6,8,128,127]{3,0,2,1:T(8,128)S(1)}, f32[6,8,128,127]{3,0,2,1:T(8,128)}, u32[]{:S(2)}) copy-start(f32[6,8,128,127]{3,0,2,1:T(8,128)} %get-tuple-element.270) | copy-start | bytes 9363460
  157.1 8.6 %copy-start.10 = (s32[1,128,8]{1,2,0:T(8,128)S(1)}, s32[1,128,8]{1,2,0:T(8,128)}, u32[]{:S(2)}) copy-start(s32[1,128,8]{1,2,0:T(8,128)} %param.18) | copy-start | bytes 12292
  165.9 8.2 %copy-start.1 = (f32[1,6,8,128,128]{4,1,3,2,0:T(8,128)S(1)}, f32[1,6,8,128,128]{4,1,3,2,0:T(8,128)}, u32[]{:S(2)}) copy-start(f32[1,6,8,128,128]{4,1,3,2,0:T(8,128)} %copy.1974) | copy-start | bytes 9437188
  165.9 8.2 %copy-start.4 = (f32[1,6,8,128,128]{4,3,2,1,0:T(8,128)S(1)}, f32[1,6,8,128,128]{4,3,2,1,0:T(8,128)}, u32[]{:S(2)}) copy-start(f32[1,6,8,128,128]{4,3,2,1,0:T(8,128)} %param.12) | copy-start | bytes 9437188
  165.9 8.2 %copy-start.6 = (f32[1,8,128,128]{3,2,1,0:T(8,128)S(1)}, f32[1,8,128,128]{3,2,1,0:T(8,128)}, u32[]{:S(2)}) copy-start(f32[1,8,128,128]{3,2,1,0:T(8,128)} %param.13) | copy-start | bytes 1572868
  222.3 16.9 %collective-permute-start.2 = (f32[6,1,128,128]{3,0,2,1:T(8,128)S(1)}, f32[6,1,128,128]{3,0,2,1:T(8,128)S(1)}, u32[]{:S(2)}, u32[]{:S(2)}) collective-permute-start(f32[6,1,128,128]{3,0,2,1:T(8,128)S(1)} %get-tuple-element.137), channel_id=1, source_target_pairs={{1,0},{2,1},{3,2},{4,3},{5,4},{6,5},{7,6},{8,7},{9,8},{10,9},{11,1... | collective-permute-start | bytes 1179656 | tf_op jit(solution)/shard_map/ppermute | solution.py:20
  230.3 14.7 %collective-permute-start.3 = (f32[6,1,128,128]{3,0,2,1:T(8,128)S(1)}, f32[6,1,128,128]{3,0,2,1:T(8,128)S(1)}, u32[]{:S(2)}, u32[]{:S(2)}) collective-permute-start(f32[6,1,128,128]{3,0,2,1:T(8,128)S(1)} %get-tuple-element.136), channel_id=1, source_target_pairs={{0,1},{1,2},{2,3},{3,4},{4,5},{5,6},{6,7},{7,8},{8,9},{9,10},{10,1... | collective-permute-start | bytes 1179656 | tf_op jit(solution)/shard_map/ppermute | solution.py:18
  239.2 5.9 %copy-start.7 = (f32[1,8,128,128]{3,2,1,0:T(8,128)S(1)}, f32[1,8,128,128]{3,2,1,0:T(8,128)}, u32[]{:S(2)}) copy-start(f32[1,8,128,128]{3,2,1,0:T(8,128)} %param.13) | copy-start | bytes 1572868
  245.0 14.1 %copy-start.2 = (f32[1,6,8,128,128]{4,1,3,2,0:T(8,128)S(1)}, f32[1,6,8,128,128]{4,1,3,2,0:T(8,128)}, u32[]{:S(2)}) copy-start(f32[1,6,8,128,128]{4,1,3,2,0:T(8,128)} %copy.1974) | copy-start | bytes 9437188
  364.1 55.6 %all-to-all-start.1 = ((f32[128,6,1,8,128]{4,3,1,2,0:T(8,128)}), f32[128,6,1,8,128]{4,3,1,2,0:T(8,128)}, u32[]{:S(2)}, u32[]{:S(2)}) async-start(f32[128,6,1,8,128]{4,3,1,2,0:T(8,128)} %constant_dynamic-update-slice_fusion.128), calls=%async_computation.1 | async-start | bytes 6291456 | tf_op jit(solution)/shard_map/all_to_all | solution.py:36
